TPU v7x, 512 devices: a whole 4x8x8 slice. The times are simulated.
512 devices in a mesh: seq: 64 (over z, y_lo, core), head: 8 (over y_hi, x).
Axes of the slice: x: 4, y: 8 (y_hi: 2, y_lo: 4; y = y_hi * 4 + y_lo), z: 8, core: 2. Of those that a mesh axis runs over, the one named last changes fastest.
Arguments:
- query_in: bfloat16 [24576, 2048], P('seq', 'head'), may hold values from -6 to 6
- key_in: bfloat16 [24576, 2048], P('seq', 'head'), may hold values from -6 to 6
- value_in: bfloat16 [24576, 2048], P('seq', 'head'), may hold values from -6 to 6
- text_keys: bfloat16 [256, 2048], P(None, 'head'), may hold values from -6 to 6
- text_values: bfloat16 [256, 2048], P(None, 'head'), may hold values from -6 to 6
- text_mask: int32 [256], replicated, may hold values 0 or 1
- window_reach: int32 [16, 2], P('head'), may hold values from 0 to 1
- tile_map: int32 [64, 3], replicated, may hold values from 0 to 14, as said below
- out_weight: bfloat16 [2048, 3072], P('head'), may hold values from -0.125 to 0.125
- gate_scale: float32 [3072], replicated, may hold values from -4 to 4
- grad_out: bfloat16 [24576, 3072], P('seq', 'head'), may hold values from -12 to 12
Outputs:
- grad_query: bfloat16 [24576, 2048], P('seq', 'head')
- grad_key: bfloat16 [24576, 2048], P('seq', 'head')
- grad_value: bfloat16 [24576, 2048], P('seq', 'head')
- grad_text_keys: bfloat16 [256, 2048], P(None, 'head')
- grad_text_values: bfloat16 [256, 2048], P(None, 'head')
- grad_gate: float32 [3072], replicated
Inputs may be any that keep to these rules, and one draw needn't show every extreme that they name: `tile_map`: index i of seq sits at grid row i // 8 and grid column i % 8. Its tile row is that grid row, or 7 minus it, plus an offset; its tile column is the grid column, or 7 minus it, plus an offset; the mirroring and the offsets are the same for all indices, and so is the frame coordinate. Of the two offsets, the one of the longer grid dimension (rows when they are equal) is 7, the other 0.
All inputs are finite; a program needn't handle non-finite values.
Results may differ from a plain program's by a relative error of at most 0.02035.
The roundings to bfloat16 on the way count: a program that leaves them out, or rounds other values in their place, can miss the bound.
Values may be sent and summed in bfloat16 or wider, within the bound.
No kernel may reach another device: no remote copies, remote signals or barrier semaphores. Data moves between devices by JAX's collectives and lax.ppermute only.
A program may use at most 64 MiB of HBM per device.

v0:
```python
import jax
import jax.numpy as jnp
import numpy as np
from jax import lax
from jax.sharding import PartitionSpec as P

HEAD_DIM = 128
TILE_T = 6
TILE_H = 8
TILE_W = 8
COLS = 8
theta_base = 256.0


def from_behind(array, axis, by):
    length = lax.axis_size(axis)
    pairs = [(i, i + by) for i in range(length) if 0 <= i + by < length]
    return lax.ppermute(array, axis, pairs)


def sections(head_dim):
    first = head_dim // 8
    second = (head_dim - first) // 2
    return ((0, first), (first, second), (first + second, second))


def rotate(values, frame_pos, row_pos, col_pos, direction):
    pieces = []
    for (offset, length), where_pos in zip(
        sections(values.shape[-1]), (frame_pos, row_pos, col_pos)
    ):
        half_len = length // 2
        freqs = theta_base ** (-2.0 * jnp.arange(half_len, dtype=jnp.float32) / length)
        angles = where_pos.astype(jnp.float32)[:, None] * freqs[None, :]
        cosine = jnp.cos(angles)[:, None, :]
        sine_part = jnp.sin(angles)[:, None, :]
        first_half = values[..., offset : offset + half_len]
        second_half = values[..., offset + half_len : offset + length]
        pieces.append(first_half * cosine - direction * second_half * sine_part)
        pieces.append(direction * first_half * sine_part + second_half * cosine)
    return jnp.concatenate(pieces, axis=-1)


def local_positions(tile_coords):
    local_index = jnp.arange(TILE_T * TILE_H * TILE_W, dtype=jnp.int32)
    plane_size = TILE_H * TILE_W
    frame_pos = tile_coords[:, 0:1] * TILE_T + (local_index // plane_size)[None, :]
    row_pos = tile_coords[:, 1:2] * TILE_H + (local_index // TILE_W % TILE_H)[None, :]
    col_pos = tile_coords[:, 2:3] * TILE_W + (local_index % TILE_W)[None, :]
    return (frame_pos.reshape(-1), row_pos.reshape(-1), col_pos.reshape(-1))


def head_scores(queries, key_block, score_scale):
    return (
        jnp.einsum("qhd,khd->hqk", queries, key_block, preferred_element_type=jnp.float32)
        * score_scale
    )


def merge_stats(running_max, running_sum, scores):
    new_max = jnp.maximum(running_max, jnp.max(scores, axis=-1))
    new_sum = running_sum * jnp.exp(running_max - new_max) + jnp.sum(
        jnp.exp(scores - new_max[..., None]), axis=-1
    )
    return (new_max, new_sum)


def on_device(
    query_in,
    key_in,
    value_in,
    text_keys,
    text_values,
    text_mask,
    window_reach,
    tile_map,
    out_weight,
    gate_scale,
    grad_out,
):
    tile_rows = query_in.shape[0]
    feature_width = query_in.shape[1]
    head_count = feature_width // HEAD_DIM
    text_count = text_keys.shape[0]
    row_count = lax.axis_size("seq") // COLS
    device = lax.axis_index("seq")
    score_scale = HEAD_DIM ** (-0.5)
    split_shape = (tile_rows, head_count, HEAD_DIM)
    own_coords = tile_map[device]
    frame_pos, row_pos, col_pos = local_positions(own_coords[None, :])
    queries = rotate(
        query_in.astype(jnp.float32).reshape(split_shape), frame_pos, row_pos, col_pos, 1.0
    ).astype(jnp.bfloat16)
    keys_rot = rotate(
        key_in.astype(jnp.float32).reshape(split_shape), frame_pos, row_pos, col_pos, 1.0
    ).astype(jnp.bfloat16)
    packed = jnp.stack([keys_rot.reshape(tile_rows, feature_width), value_in])
    row_steps = np.array([-1, -1, -1, 0, 0, 0, 1, 1, 1], dtype=np.int32)
    col_steps = np.array([-1, 0, 1, -1, 0, 1, -1, 0, 1], dtype=np.int32)
    fetched = []
    for number in range(9):
        if number == 4:
            fetched.append(packed)
        else:
            fetched.append(
                from_behind(packed, "seq", int(row_steps[number]) * COLS + int(col_steps[number]))
            )
    blocks = jnp.stack(fetched)
    source_row = device // COLS - jnp.asarray(row_steps)
    source_col = device % COLS - jnp.asarray(col_steps)
    usable_block = (
        (source_row >= 0) & (source_row < row_count) & (source_col >= 0) & (source_col < COLS)
    )
    source = jnp.clip(source_row, 0, row_count - 1) * COLS + jnp.clip(source_col, 0, COLS - 1)
    near_coords = tile_map[source]
    row_gap = jnp.abs(near_coords[:, 1] - own_coords[1])
    col_gap = jnp.abs(near_coords[:, 2] - own_coords[2])
    allowed = (
        usable_block[None, :]
        & (row_gap[None, :] <= window_reach[:, 0:1])
        & (col_gap[None, :] <= window_reach[:, 1:2])
    )
    allow_rows = allowed.T
    text_open = (text_mask == 1)[None, None, :]
    block_keys = blocks[:, 0].reshape(9, tile_rows, head_count, HEAD_DIM)
    block_values = blocks[:, 1].reshape(9, tile_rows, head_count, HEAD_DIM)
    text_key_split = text_keys.reshape(text_count, head_count, HEAD_DIM)
    text_value_split = text_values.reshape(text_count, head_count, HEAD_DIM)

    def stats_step(carry, inputs):
        key_block, allow = inputs
        scores = jnp.where(
            allow[:, None, None], head_scores(queries, key_block, score_scale), -jnp.inf
        )
        return (merge_stats(carry[0], carry[1], scores), None)

    start_stats = (
        jnp.full((head_count, tile_rows), -1e30, jnp.float32),
        jnp.zeros((head_count, tile_rows), jnp.float32),
    )
    (running_max, running_sum), _ = lax.scan(stats_step, start_stats, (block_keys, allow_rows))
    text_scores = jnp.where(text_open, head_scores(queries, text_key_split, score_scale), -jnp.inf)
    running_max, running_sum = merge_stats(running_max, running_sum, text_scores)
    log_norm = running_max + jnp.log(running_sum)

    def weights_for(key_block, allow_mask):
        scores = head_scores(queries, key_block, score_scale)
        return jnp.where(allow_mask, jnp.exp(scores - log_norm[:, :, None]), 0.0)

    def output_step(total_out, inputs):
        key_block, value_block, allow = inputs
        probs = weights_for(key_block, allow[:, None, None]).astype(jnp.bfloat16)
        return (
            total_out
            + jnp.einsum("hqk,khd->hqd", probs, value_block, preferred_element_type=jnp.float32),
            None,
        )

    total_out, _ = lax.scan(
        output_step,
        jnp.zeros((head_count, tile_rows, HEAD_DIM), jnp.float32),
        (block_keys, block_values, allow_rows),
    )
    text_probs = weights_for(text_key_split, text_open).astype(jnp.bfloat16)
    total_out = total_out + jnp.einsum(
        "hqk,khd->hqd", text_probs, text_value_split, preferred_element_type=jnp.float32
    )
    attn = total_out.transpose(1, 0, 2).reshape(tile_rows, feature_width).astype(jnp.bfloat16)
    piece = lax.all_gather(grad_out, "head", axis=1, tiled=True)
    grad_proj = (piece.astype(jnp.float32) * gate_scale[None, :]).astype(jnp.bfloat16)
    grad_acc = lax.dot_general(
        grad_proj, out_weight, (((1,), (1,)), ((), ())), preferred_element_type=jnp.float32
    )
    projected = jnp.dot(attn, out_weight, preferred_element_type=jnp.float32)
    terms = jnp.sum(piece.astype(jnp.float32) * projected, axis=0)
    gate_terms = terms
    grad_attn, gate_terms = (grad_acc, gate_terms)
    grad_heads = grad_attn.astype(jnp.bfloat16).reshape(split_shape)
    delta = jnp.sum(
        grad_heads.astype(jnp.float32) * attn.reshape(split_shape).astype(jnp.float32), axis=-1
    ).T

    def grad_block(key_block, value_block, allow_mask):
        weights = weights_for(key_block, allow_mask)
        grad_weights = jnp.einsum(
            "qhd,khd->hqk", grad_heads, value_block, preferred_element_type=jnp.float32
        )
        grad_scores = (weights * (grad_weights - delta[:, :, None])).astype(jnp.bfloat16)
        query_part = jnp.einsum(
            "hqk,khd->hqd", grad_scores, key_block, preferred_element_type=jnp.float32
        )
        key_part = (
            jnp.einsum("hqk,qhd->khd", grad_scores, queries, preferred_element_type=jnp.float32)
            * score_scale
        )
        value_part = jnp.einsum(
            "hqk,qhd->khd",
            weights.astype(jnp.bfloat16),
            grad_heads,
            preferred_element_type=jnp.float32,
        )
        return (query_part, key_part, value_part)

    text_query_part, text_key_part, text_value_part = grad_block(
        text_key_split, text_value_split, text_open
    )
    text_key_grad = text_key_part.reshape(text_count, feature_width)
    text_value_grad = text_value_part.reshape(text_count, feature_width)

    def back_step(query_acc, inputs):
        key_block, value_block, allow = inputs
        query_part, key_part, value_part = grad_block(key_block, value_block, allow[:, None, None])
        stacked = jnp.stack(
            [
                key_part.reshape(tile_rows, feature_width),
                value_part.reshape(tile_rows, feature_width),
            ]
        )
        return (query_acc + query_part, stacked)

    query_acc, partials = lax.scan(
        back_step,
        jnp.zeros((head_count, tile_rows, HEAD_DIM), jnp.float32),
        (block_keys, block_values, allow_rows),
    )
    own_total = partials[4]
    for number in range(9):
        if number != 4:
            own_total = own_total + from_behind(
                partials[number].astype(jnp.bfloat16),
                "seq",
                -(int(row_steps[number]) * COLS + int(col_steps[number])),
            ).astype(jnp.float32)
    query_acc = query_acc + text_query_part
    text_key_sum, text_value_sum = lax.psum((text_key_grad, text_value_grad), "seq")
    grad_gate = lax.psum(gate_terms, ("seq", "head"))
    grad_query = (
        rotate((query_acc * score_scale).transpose(1, 0, 2), frame_pos, row_pos, col_pos, -1.0)
        .astype(jnp.bfloat16)
        .reshape(tile_rows, feature_width)
    )
    grad_key = (
        rotate(own_total[0].reshape(split_shape), frame_pos, row_pos, col_pos, -1.0)
        .astype(jnp.bfloat16)
        .reshape(tile_rows, feature_width)
    )
    grad_value = own_total[1].astype(jnp.bfloat16)
    return (
        grad_query,
        grad_key,
        grad_value,
        text_key_sum.astype(jnp.bfloat16),
        text_value_sum.astype(jnp.bfloat16),
        grad_gate,
    )


def solution(mesh):
    placed = (
        P("seq", "head"),
        P("seq", "head"),
        P("seq", "head"),
        P(None, "head"),
        P(None, "head"),
        P(),
        P("head", None),
        P(),
        P("head", None),
        P(),
        P("seq", "head"),
    )
    return jax.shard_map(
        on_device,
        mesh=mesh,
        in_specs=placed,
        out_specs=(
            P("seq", "head"),
            P("seq", "head"),
            P("seq", "head"),
            P(None, "head"),
            P(None, "head"),
            P(),
        ),
        check_vma=False,
    )
```

profile of v0, /device:TPU:2, one launch (start us, length us, event | category | flops | bytes accessed | tf_op | source)
XLA Modules:
  0.0 668.5 jit_solution(16040238661851726279)
XLA Ops:
  18.0 1.8 copy.175
  25.4 1.7 copy.171
  27.2 2.4 broadcast_multiply_fusion
  29.5 2.1 add_convert_fusion.8
  32.2 2.1 concatenate.16
  36.2 5.0 collective-permute-start.6
  41.2 5.4 collective-permute-start.5
  46.7 2.0 collective-permute-start.4
  55.3 1.7 copy.182
  57.0 1.5 copy.135
  58.5 1.4 concatenate.17
  60.1 1.4 gather_fusion
  61.6 1.8 select_reduce_fusion
  66.2 3.7 collective-permute-done
  74.5 15.0 %collective-permute-done.2 = bf16[2,384,256]{1,2,0:T(8,128)(2,1)S(1)} collective-permute-done((bf16[2,384,256]{1,2,0:T(8,128)(2,1)}, bf16[2,384,256]{1,2,0:T(8,128)(2,1)S(1)}, u32[]{:S(2)}, u32[]{:S(2)}) %collective-permute-start.2) | collective-permute-done | bytes 393248 | tf_op jit(solution)/shard_map/ppermute | solution.py:18
  89.5 1.5 collective-permute-start.7
  94.5 1.9 collective-permute-done.7
  96.5 2.3 fusion.93
  98.8 3.8 copy.126
  102.6 13.8 %while.37 = (s32[]{:T(128)}, f32[2,384]{1,0:T(2,128)S(1)}, f32[2,384]{1,0:T(2,128)S(1)}, pred[9,2]{1,0:T(8,128)(4,1)S(1)}, bf16[9,384,2,128]{3,1,2,0:T(8,128)(2,...) while((s32[]{:T(128)}, f32[2,384]{1,0:T(2,128)S(1)}, f32[2,384]{1,0:T(2,128)S(1)}, ...), condition=%wide.region_3.4_spmd.clone, body=%wide.region_0.3_spmd.clone.sunk | while | flops 76975872 | bytes 2792566 | solution.py:141
  117.0 3.9 copy.128
  121.2 29.6 %while.38 = (s32[]{:T(128)}, f32[2,384,128]{2,1,0:T(8,128)}, pred[9,2]{1,0:T(8,128)(4,1)}, bf16[9,384,2,128]{3,1,2,0:T(8,128)(2,1)}, bf16[384,2,128]{2,0,1:T(8,1...) while((s32[]{:T(128)}, f32[2,384,128]{2,1,0:T(8,128)}, ...), condition=%wide.region_7.8_spmd.clone, body=%wide.region_6.7_spmd.clone.sunk | while | flops 152371200 | bytes 1380984 | solution.py:159
  121.9 2.4 fusion.151
  125.0 2.6 fusion.151
  128.3 2.6 fusion.151
  131.6 2.6 fusion.151
  134.9 2.6 fusion.151
  138.2 2.6 fusion.151
  141.5 2.6 fusion.151
  144.8 2.6 fusion.151
  148.1 2.6 fusion.151
  150.8 1.9 copy.125
  152.7 2.7 fusion.53
  158.5 55.7 %while.39 = (s32[]{:T(128)}, f32[2,384,128]{2,1,0:T(8,128)S(1)}, f32[9,2,384,256]{2,3,1,0:T(8,128)}, pred[9,2]{1,0:T(8,128)(4,1)}, bf16[9,384,2,128]{3,1,2,0:T(8...) while((s32[]{:T(128)}, f32[2,384,128]{2,1,0:T(8,128)S(1)}, ...), condition=%wide.region_10.11_spmd.clone, body=%wide.region_9.10_spmd.clone.sunk | while | flops 380043264 | bytes 9836705 | solution.py:221
  162.0 1.4 convolution_add_fusion.4
  214.2 3.6 convert.109
  217.7 1.8 slice_bitcast_fusion.7
  219.5 5.7 collective-permute-start.8
  229.9 1.8 copy.146
  234.3 2.5 fusion.45
  236.9 126.0 %psum.23 = f32[3072]{0:T(1024)} all-reduce(f32[3072]{0:T(1024)S(1)} %fusion.45), channel_id=1, replica_groups=mesh['seq'=64,'head'=8] {'seq','head'}, use_global_device_ids=true, to_apply=%region_14.15 | all-reduce | flops 3072 | bytes 24576 | tf_op jit(solution)/shard_map/psum | solution.py:236
  362.9 2.5 collective-permute-start.11
  365.4 7.6 %collective-permute-start.10 = (bf16[2,384,256]{1,2,0:T(8,128)(2,1)}, bf16[2,384,256]{1,2,0:T(8,128)(2,1)}, u32[]{:S(2)}, u32[]{:S(2)}) collective-permute-start(bf16[2,384,256]{1,2,0:T(8,128)(2,1)} %get-tuple-element.347), channel_id=1, source_target_pairs={{0,56},{8,64},{16,72},{24,80},{32,88},{40,96},{48,104},{56,112},{6... | collective-permute-start | bytes 1179656 | tf_op jit(solution)/shard_map/ppermute | solution.py:18
  373.0 2.4 collective-permute-start.9
  375.7 269.2 %all-reduce.2 = (bf16[256,256]{1,0:T(8,128)(2,1)}, bf16[256,256]{1,0:T(8,128)(2,1)}) all-reduce(f32[256,256]{1,0:T(8,128)} %copy.146, f32[256,256]{1,0:T(8,128)S(1)} %copy.148), channel_id=1, replica_groups=mesh['seq'=64,'head'=8] {'seq'}, use_global_device_ids=true, to_apply=%region_11.12 | all-reduce | flops 131072 | bytes 786432 | tf_op jit(solution)/shard_map/psum | solution.py:235
  644.9 2.5 fusion.63
  653.8 2.2 add_convert_fusion.2
  657.4 1.6 concatenate.18
  (296 shorter events, 130.0 us)
Async XLA Ops:
  7.2 145.5 %copy-start = (bf16[256,3072]{1,0:T(8,128)(2,1)S(1)}, bf16[256,3072]{1,0:T(8,128)(2,1)}, u32[]{:S(2)}) copy-start(bf16[256,3072]{1,0:T(8,128)(2,1)} %param.27) | copy-start | bytes 4718596
  7.2 4.3 copy-start.31
  7.2 7.7 %copy-start.28 = (bf16[384,256]{1,0:T(8,128)(2,1)S(1)}, bf16[384,256]{1,0:T(8,128)(2,1)}, u32[]{:S(2)}) copy-start(bf16[384,256]{1,0:T(8,128)(2,1)} %param.21) | copy-start | bytes 589828
  7.2 145.5 %all-gather.2.cloned.1.call-start = ((), (), s32[]{:S(2)}) async-start(), calls=%async_computation | async-start | bytes 2654208 | tf_op jit(solution)/shard_map/all_gather | solution.py:169
  14.8 14.8 %copy-start.6 = (f32[384,8]{1,0:T(8,128)}, f32[384,8]{1,0:T(8,128)S(1)}, u32[]{:S(2)}) copy-start(f32[384,8]{1,0:T(8,128)S(1)} %copy.103) | copy-start | bytes 36868
  27.1 4.5 copy-start.9
  27.1 4.5 copy-start.10
  27.1 4.5 copy-start.11
  27.1 4.5 copy-start.12
  27.1 4.5 copy-start.13
  27.1 4.5 copy-start.14
  27.1 4.5 copy-start.15
  27.1 4.5 copy-start.16
  29.5 2.7 copy-start.2
  32.2 21.0 %copy-start.32 = (s32[2,2]{1,0:T(2,128)S(1)}, s32[2,2]{1,0:T(2,128)}, u32[]{:S(2)}) copy-start(s32[2,2]{1,0:T(2,128)} %param.25) | copy-start | bytes 52
  35.4 23.1 %copy-start.4 = (bf16[384,2,128]{0,2,1:T(8,128)(2,1)}, bf16[384,2,128]{0,2,1:T(8,128)(2,1)S(1)}, u32[]{:S(2)}) copy-start(bf16[384,2,128]{0,2,1:T(8,128)(2,1)S(1)} %copy.110) | copy-start | bytes 589828
  36.2 57.2 %collective-permute-start.6 = (bf16[2,384,256]{1,2,0:T(8,128)(2,1)}, bf16[2,384,256]{1,2,0:T(8,128)(2,1)}, u32[]{:S(2)}, u32[]{:S(2)}) collective-permute-start(bf16[2,384,256]{1,2,0:T(8,128)(2,1)} %pad_maximum_fusion), channel_id=1, source_target_pairs={{0,64},{8,72},{16,80},{24,88},{32,96},{40,104},{48,112},{56,120},{... | collective-permute-start | bytes 1179656 | tf_op jit(solution)/shard_map/ppermute | solution.py:18
  41.2 51.1 %collective-permute-start.5 = (bf16[2,384,256]{1,2,0:T(8,128)(2,1)}, bf16[2,384,256]{1,2,0:T(8,128)(2,1)}, u32[]{:S(2)}, u32[]{:S(2)}) collective-permute-start(bf16[2,384,256]{1,2,0:T(8,128)(2,1)} %pad_maximum_fusion), channel_id=1, source_target_pairs={{0,56},{8,64},{16,72},{24,80},{32,88},{40,96},{48,104},{56,112},{6... | collective-permute-start | bytes 1179656 | tf_op jit(solution)/shard_map/ppermute | solution.py:18
  46.7 44.6 %collective-permute-start.4 = (bf16[2,384,256]{1,2,0:T(8,128)(2,1)}, bf16[2,384,256]{1,2,0:T(8,128)(2,1)}, u32[]{:S(2)}, u32[]{:S(2)}) collective-permute-start(bf16[2,384,256]{1,2,0:T(8,128)(2,1)} %pad_maximum_fusion), channel_id=1, source_target_pairs={{0,8},{8,16},{16,24},{24,32},{32,40},{40,48},{48,56},{56,64},{64,7... | collective-permute-start | bytes 1179656 | tf_op jit(solution)/shard_map/ppermute | solution.py:18
  48.7 23.5 %collective-permute-start.1 = (bf16[2,384,256]{1,2,0:T(8,128)(2,1)}, bf16[2,384,256]{1,2,0:T(8,128)(2,1)}, u32[]{:S(2)}, u32[]{:S(2)}) collective-permute-start(bf16[2,384,256]{1,2,0:T(8,128)(2,1)} %pad_maximum_fusion), channel_id=1, source_target_pairs={{64,0},{72,8},{80,16},{88,24},{96,32},{104,40},{112,48},{120,56},{... | collective-permute-start | bytes 1179656 | tf_op jit(solution)/shard_map/ppermute | solution.py:18
  50.0 19.8 %collective-permute-start = (bf16[2,384,256]{1,2,0:T(8,128)(2,1)}, bf16[2,384,256]{1,2,0:T(8,128)(2,1)}, u32[]{:S(2)}, u32[]{:S(2)}) collective-permute-start(bf16[2,384,256]{1,2,0:T(8,128)(2,1)} %pad_maximum_fusion), channel_id=1, source_target_pairs={{72,0},{80,8},{88,16},{96,24},{104,32},{112,40},{120,48},{128,56},... | collective-permute-start | bytes 1179656 | tf_op jit(solution)/shard_map/ppermute | solution.py:18
  63.4 27.8 %copy-start.5 = (bf16[384,2,128]{0,2,1:T(8,128)(2,1)S(1)}, bf16[384,2,128]{0,2,1:T(8,128)(2,1)}, u32[]{:S(2)}) copy-start(bf16[384,2,128]{0,2,1:T(8,128)(2,1)} %copy-done.4) | copy-start | bytes 589828
  69.8 19.7 %collective-permute-start.2 = (bf16[2,384,256]{1,2,0:T(8,128)(2,1)}, bf16[2,384,256]{1,2,0:T(8,128)(2,1)S(1)}, u32[]{:S(2)}, u32[]{:S(2)}) collective-permute-start(bf16[2,384,256]{1,2,0:T(8,128)(2,1)} %pad_maximum_fusion), channel_id=1, source_target_pairs={{56,0},{64,8},{72,16},{80,24},{88,32},{96,40},{104,48},{112,56},{1... | collective-permute-start | bytes 1179656 | tf_op jit(solution)/shard_map/ppermute | solution.py:18
  72.2 19.0 %collective-permute-start.3 = (bf16[2,384,256]{1,2,0:T(8,128)(2,1)}, bf16[2,384,256]{1,2,0:T(8,128)(2,1)S(1)}, u32[]{:S(2)}, u32[]{:S(2)}) collective-permute-start(bf16[2,384,256]{1,2,0:T(8,128)(2,1)} %pad_maximum_fusion), channel_id=1, source_target_pairs={{8,0},{16,8},{24,16},{32,24},{40,32},{48,40},{56,48},{64,56},{72,6... | collective-permute-start | bytes 1179656 | tf_op jit(solution)/shard_map/ppermute | solution.py:18
  89.5 6.9 %collective-permute-start.7 = (bf16[2,384,256]{1,2,0:T(8,128)(2,1)}, bf16[2,384,256]{1,2,0:T(8,128)(2,1)S(1)}, u32[]{:S(2)}, u32[]{:S(2)}) collective-permute-start(bf16[2,384,256]{1,2,0:T(8,128)(2,1)} %pad_maximum_fusion), channel_id=1, source_target_pairs={{0,72},{8,80},{16,88},{24,96},{32,104},{40,112},{48,120},{56,128},... | collective-permute-start | bytes 1179656 | tf_op jit(solution)/shard_map/ppermute | solution.py:18
  117.0 3.9 copy-start.30
  117.0 3.9 copy-start.29
  152.7 3.8 copy-start.8
  152.7 3.8 copy-start.26
  217.7 10.1 %copy-start.1 = (bf16[2,384,256]{1,2,0:T(8,128)(2,1)S(1)}, bf16[2,384,256]{1,2,0:T(8,128)(2,1)}, u32[]{:S(2)}) copy-start(bf16[2,384,256]{1,2,0:T(8,128)(2,1)} %fusion.50) | copy-start | bytes 1179652
  219.5 14.8 %copy-start.27 = (bf16[2,384,128]{1,2,0:T(8,128)(2,1)S(1)}, bf16[2,384,128]{1,2,0:T(8,128)(2,1)}, u32[]{:S(2)}) copy-start(bf16[2,384,128]{1,2,0:T(8,128)(2,1)} %get-tuple-element.425) | copy-start | bytes 589828
  219.5 143.4 %collective-permute-start.8 = (bf16[2,384,256]{1,2,0:T(8,128)(2,1)}, bf16[2,384,256]{1,2,0:T(8,128)(2,1)}, u32[]{:S(2)}, u32[]{:S(2)}) collective-permute-start(bf16[2,384,256]{1,2,0:T(8,128)(2,1)} %get-tuple-element.341), channel_id=1, source_target_pairs={{0,72},{8,80},{16,88},{24,96},{32,104},{40,112},{48,120},{56,128},... | collective-permute-start | bytes 1179656 | tf_op jit(solution)/shard_map/ppermute | solution.py:18
  225.3 140.1 %collective-permute-start.15 = (bf16[2,384,256]{1,2,0:T(8,128)(2,1)}, bf16[2,384,256]{1,2,0:T(8,128)(2,1)}, u32[]{:S(2)}, u32[]{:S(2)}) collective-permute-start(bf16[2,384,256]{1,2,0:T(8,128)(2,1)} %get-tuple-element.342), channel_id=1, source_target_pairs={{72,0},{80,8},{88,16},{96,24},{104,32},{112,40},{120,48},{128,56},... | collective-permute-start | bytes 1179656 | tf_op jit(solution)/shard_map/ppermute | solution.py:18
  226.5 146.4 %collective-permute-start.14 = (bf16[2,384,256]{1,2,0:T(8,128)(2,1)}, bf16[2,384,256]{1,2,0:T(8,128)(2,1)}, u32[]{:S(2)}, u32[]{:S(2)}) collective-permute-start(bf16[2,384,256]{1,2,0:T(8,128)(2,1)} %get-tuple-element.343), channel_id=1, source_target_pairs={{64,0},{72,8},{80,16},{88,24},{96,32},{104,40},{112,48},{120,56},{... | collective-permute-start | bytes 1179656 | tf_op jit(solution)/shard_map/ppermute | solution.py:18
  231.7 413.2 %collective-permute-start.13 = (bf16[2,384,256]{1,2,0:T(8,128)(2,1)}, bf16[2,384,256]{1,2,0:T(8,128)(2,1)}, u32[]{:S(2)}, u32[]{:S(2)}) collective-permute-start(bf16[2,384,256]{1,2,0:T(8,128)(2,1)} %get-tuple-element.344), channel_id=1, source_target_pairs={{56,0},{64,8},{72,16},{80,24},{88,32},{96,40},{104,48},{112,56},{1... | collective-permute-start | bytes 1179656 | tf_op jit(solution)/shard_map/ppermute | solution.py:18
  233.0 411.9 %collective-permute-start.12 = (bf16[2,384,256]{1,2,0:T(8,128)(2,1)}, bf16[2,384,256]{1,2,0:T(8,128)(2,1)}, u32[]{:S(2)}, u32[]{:S(2)}) collective-permute-start(bf16[2,384,256]{1,2,0:T(8,128)(2,1)} %get-tuple-element.345), channel_id=1, source_target_pairs={{8,0},{16,8},{24,16},{32,24},{40,32},{48,40},{56,48},{64,56},{72,6... | collective-permute-start | bytes 1179656 | tf_op jit(solution)/shard_map/ppermute | solution.py:18
  234.3 141.0 %copy-start.21 = (bf16[256,256]{0,1:T(8,128)(2,1)S(1)}, bf16[256,256]{0,1:T(8,128)(2,1)}, u32[]{:S(2)}) copy-start(bf16[256,256]{0,1:T(8,128)(2,1)} %copy.182) | copy-start | bytes 393220
  362.9 282.0 %collective-permute-start.11 = (bf16[2,384,256]{1,2,0:T(8,128)(2,1)}, bf16[2,384,256]{1,2,0:T(8,128)(2,1)}, u32[]{:S(2)}, u32[]{:S(2)}) collective-permute-start(bf16[2,384,256]{1,2,0:T(8,128)(2,1)} %get-tuple-element.346), channel_id=1, source_target_pairs={{0,8},{8,16},{16,24},{24,32},{32,40},{40,48},{48,56},{56,64},{64,7... | collective-permute-start | bytes 1179656 | tf_op jit(solution)/shard_map/ppermute | solution.py:18
  365.4 279.6 %collective-permute-start.10 = (bf16[2,384,256]{1,2,0:T(8,128)(2,1)}, bf16[2,384,256]{1,2,0:T(8,128)(2,1)}, u32[]{:S(2)}, u32[]{:S(2)}) collective-permute-start(bf16[2,384,256]{1,2,0:T(8,128)(2,1)} %get-tuple-element.347), channel_id=1, source_target_pairs={{0,56},{8,64},{16,72},{24,80},{32,88},{40,96},{48,104},{56,112},{6... | collective-permute-start | bytes 1179656 | tf_op jit(solution)/shard_map/ppermute | solution.py:18
  373.0 272.0 %collective-permute-start.9 = (bf16[2,384,256]{1,2,0:T(8,128)(2,1)}, bf16[2,384,256]{1,2,0:T(8,128)(2,1)}, u32[]{:S(2)}, u32[]{:S(2)}) collective-permute-start(bf16[2,384,256]{1,2,0:T(8,128)(2,1)} %get-tuple-element.348), channel_id=1, source_target_pairs={{0,64},{8,72},{16,80},{24,88},{32,96},{40,104},{48,112},{56,120},{... | collective-permute-start | bytes 1179656 | tf_op jit(solution)/shard_map/ppermute | solution.py:18
  648.2 5.6 copy-start.7
  652.0 4.1 copy-start.3
  652.0 4.1 copy-start.22
  653.8 2.2 copy-start.17
  653.8 2.2 copy-start.18
  653.8 2.2 copy-start.19
  657.4 2.6 copy-start.24
  657.4 2.6 copy-start.25
  (3 other events, 5.0 us)
Sparse Core Ops, SparseCore 0:
  51.4 93.9 all-gather.1
where the time goes:
time: 672 us; the launch traced here: 668 us
  blocking collectives  395 us (59%)
  matrix products  86.9 us (13%)
  local copies, waits for them, and re-layouts  73.9 us (11%)
  starting transfers between devices  42.5 us (6%)
  other arithmetic  32 us (5%)
  waiting for transfers between devices  20.7 us (3%)
  between operations  16.5 us (2%)
    psum x1, blocking collectives, on_device(): lax.psum((text_key_grad, text_value_grad), 'seq')  269 us
    psum x1, blocking collectives, on_device(): grad_gate = lax.psum(gate_terms, ('seq', 'head'))  126 us
    ppermute x16, starting transfers between devices, from_behind(): return lax.ppermute(array, axis, pairs)  42.4 us
    unnamed x103, local copies, waits for them, and re-layouts  36.4 us
    dot_general x19, matrix products, head_scores(): jnp.einsum('qhd,khd->hqk', queries, key_block, preferred_element_type=jnp...  24.8 us
    dot_general x9, matrix products, output_step(): jnp.einsum('hqk,khd->hqd', probs, value_block, preferred_element_type=jnp...  23.4 us
    ppermute x16, waiting for transfers between devices, from_behind(): return lax.ppermute(array, axis, pairs)  20.7 us
  transfers between devices with their start and end apart: 17, of which 3 were waited for; matrix products, arithmetic and copies ran while one was open for 12% of the time, Pallas kernels for 0%

commit v1 on v0

--- a/solution.py
+++ b/solution.py
@@ -1,8 +1,10 @@
+import functools
 import jax
 import jax.numpy as jnp
 import numpy as np
 from jax import lax
 from jax.sharding import PartitionSpec as P
+from jax.lax import all_gather
 
 HEAD_DIM = 128
 TILE_T = 6
@@ -10,6 +12,13 @@
 TILE_W = 8
 COLS = 8
 theta_base = 256.0
+
+
+def deliver_scenes(panel, chip_axis):
+    return all_gather(panel, axis_name=chip_axis).sum(axis=0)
+
+
+advance_sections = functools.partial(deliver_scenes, chip_axis=("seq", "head"))
 
 
 def from_behind(array, axis, by):
@@ -233,7 +242,7 @@
             ).astype(jnp.float32)
     query_acc = query_acc + text_query_part
     text_key_sum, text_value_sum = lax.psum((text_key_grad, text_value_grad), "seq")
-    grad_gate = lax.psum(gate_terms, ("seq", "head"))
+    grad_gate = advance_sections(gate_terms)
     grad_query = (
         rotate((query_acc * score_scale).transpose(1, 0, 2), frame_pos, row_pos, col_pos, -1.0)
         .astype(jnp.bfloat16)

time: 672 us -> 1630 us (2.43)
  the two profiles are of different devices: /device:TPU:2 before, /device:TPU:193 now
where the time goes in v1:
time: 1630 us
  waiting for transfers between devices  1080 us (66%)
  blocking collectives  266 us (16%)
  matrix products  82.9 us (5%)
  local copies, waits for them, and re-layouts  77.7 us (5%)
  starting transfers between devices  70.4 us (4%)
  other arithmetic  35.4 us (2%)
  between operations  16.8 us (1%)
    all_gather x1, waiting for transfers between devices, deliver_scenes(): return all_gather(panel, axis_name=chip_axis).sum(axis=0)  1070 us
    psum x1, blocking collectives, on_device(): lax.psum((text_key_grad, text_value_grad), 'seq')  266 us
    ppermute x16, starting transfers between devices, from_behind(): return lax.ppermute(array, axis, pairs)  70.3 us
    unnamed x99, local copies, waits for them, and re-layouts  34.3 us
  transfers between devices with their start and end apart: 18, of which 4 were waited for; matrix products, arithmetic and copies ran while one was open for 9% of the time, Pallas kernels for 0%

profile of v1, /device:TPU:193, one launch (start us, length us, event | category | flops | bytes accessed | tf_op | source)
XLA Modules:
  0.0 1627.7 jit_solution(7356952836391466720)
XLA Ops:
  18.3 1.8 copy.281
  27.4 2.4 broadcast_multiply_fusion
  29.8 2.1 add_convert_fusion.8
  32.5 2.1 concatenate.16
  36.4 5.2 collective-permute-start.6
  41.6 3.9 collective-permute-start.5
  45.6 2.5 collective-permute-start.4
  48.1 2.2 collective-permute-start.1
  50.3 1.9 collective-permute-start
  56.2 1.7 copy.288
  62.5 1.8 select_reduce_fusion
  68.0 5.4 collective-permute-start.2
  74.4 2.0 collective-permute-start.3
  77.5 7.4 collective-permute-done.2
  84.8 5.8 collective-permute-start.7
  95.6 2.3 fusion.93
  97.9 3.9 copy.232
  101.8 13.8 while.37
  116.2 3.9 copy.234
  120.3 29.4 %while.38 = (s32[]{:T(128)}, f32[2,384,128]{2,1,0:T(8,128)}, pred[9,2]{1,0:T(8,128)(4,1)}, bf16[9,384,2,128]{3,1,2,0:T(8,128)(2,1)}, bf16[384,2,128]{2,0,1:T(8,1...) while((s32[]{:T(128)}, f32[2,384,128]{2,1,0:T(8,128)}, ...), condition=%wide.region_7.8_spmd.clone, body=%wide.region_6.7_spmd.clone.sunk | while | flops 152371200 | bytes 1380984 | solution.py:168
  121.0 2.4 fusion.151
  124.1 2.6 fusion.151
  127.4 2.6 fusion.151
  130.7 2.6 fusion.151
  134.0 2.6 fusion.151
  137.2 2.6 fusion.151
  140.5 2.6 fusion.151
  143.8 2.6 fusion.151
  147.1 2.6 fusion.151
  149.7 1.9 copy.231
  151.6 2.8 fusion.53
  157.5 55.7 %while.39 = (s32[]{:T(128)}, f32[2,384,128]{2,1,0:T(8,128)S(1)}, f32[9,2,384,256]{2,3,1,0:T(8,128)}, pred[9,2]{1,0:T(8,128)(4,1)}, bf16[9,384,2,128]{3,1,2,0:T(8...) while((s32[]{:T(128)}, f32[2,384,128]{2,1,0:T(8,128)S(1)}, ...), condition=%wide.region_10.11_spmd.clone, body=%wide.region_9.10_spmd.clone.sunk | while | flops 380043264 | bytes 9836705 | solution.py:230
  213.1 3.6 convert.109
  216.7 1.7 slice_bitcast_fusion.7
  218.4 6.7 collective-permute-start.8
  225.1 4.7 collective-permute-start.15
  229.8 2.1 collective-permute-start.14
  232.6 3.7 collective-permute-start.13
  236.3 9.9 collective-permute-start.12
  246.2 1.9 collective-permute-start.11
  248.1 7.7 collective-permute-start.10
  255.9 4.7 collective-permute-start.9
  260.9 265.6 %all-reduce.2 = (bf16[256,256]{1,0:T(8,128)(2,1)}, bf16[256,256]{1,0:T(8,128)(2,1)}) all-reduce(f32[256,256]{1,0:T(8,128)S(1)} %copy.252, f32[256,256]{1,0:T(8,128)S(1)} %copy-done.18), channel_id=1, replica_groups=mesh['seq'=64,'head'=8] {'seq'}, use_global_device_ids=true, to_apply=%region_11.12 | all-reduce | flops 131072 | bytes 786432 | tf_op jit(solution)/shard_map/psum | solution.py:244
  526.5 2.2 fusion.63
  533.6 2.1 add_convert_fusion.2
  541.3 1068.5 %all-gather.6.cloned.1.call-done = f32[1572864]{0:T(1024)} async-done(((f32[3072]{0:T(1024)}), f32[1572864]{0:T(1024)}) %all-gather.6.cloned.1.call-update) | async-done | bytes 6291472 | tf_op jit(solution)/shard_map/all_gather | solution.py:18
  1609.8 7.3 reshape.349
  1617.2 3.7 reduce_sum.48
  (296 shorter events, 128.1 us)
Async XLA Ops:
  7.2 144.4 %copy-start = (bf16[256,3072]{1,0:T(8,128)(2,1)S(1)}, bf16[256,3072]{1,0:T(8,128)(2,1)}, u32[]{:S(2)}) copy-start(bf16[256,3072]{1,0:T(8,128)(2,1)} %param.27) | copy-start | bytes 4718596
  7.2 4.3 copy-start.28
  7.2 7.9 copy-start.25
  7.2 144.4 %all-gather.4.cloned.1.call-start = ((), (), s32[]{:S(2)}) async-start(), calls=%async_computation | async-start | bytes 2654208 | tf_op jit(solution)/shard_map/all_gather | solution.py:178
  15.0 14.8 copy-start.6
  27.3 4.5 copy-start.9
  27.3 4.5 copy-start.10
  27.3 4.5 copy-start.11
  27.3 4.5 copy-start.12
  27.3 4.5 copy-start.13
  27.3 4.5 copy-start.14
  27.4 4.5 copy-start.15
  27.4 4.5 copy-start.16
  29.8 2.7 copy-start.2
  32.5 21.8 %copy-start.29 = (s32[2,2]{1,0:T(2,128)S(1)}, s32[2,2]{1,0:T(2,128)}, u32[]{:S(2)}) copy-start(s32[2,2]{1,0:T(2,128)} %param.25) | copy-start | bytes 52
  35.6 23.8 %copy-start.4 = (bf16[384,2,128]{0,2,1:T(8,128)(2,1)}, bf16[384,2,128]{0,2,1:T(8,128)(2,1)S(1)}, u32[]{:S(2)}) copy-start(bf16[384,2,128]{0,2,1:T(8,128)(2,1)S(1)} %copy.216) | copy-start | bytes 589828
  36.4 56.6 %collective-permute-start.6 = (bf16[2,384,256]{1,2,0:T(8,128)(2,1)}, bf16[2,384,256]{1,2,0:T(8,128)(2,1)}, u32[]{:S(2)}, u32[]{:S(2)}) collective-permute-start(bf16[2,384,256]{1,2,0:T(8,128)(2,1)} %pad_maximum_fusion), channel_id=1, source_target_pairs={{0,64},{8,72},{16,80},{24,88},{32,96},{40,104},{48,112},{56,120},{... | collective-permute-start | bytes 1179656 | tf_op jit(solution)/shard_map/ppermute | solution.py:27
  41.6 50.3 %collective-permute-start.5 = (bf16[2,384,256]{1,2,0:T(8,128)(2,1)}, bf16[2,384,256]{1,2,0:T(8,128)(2,1)}, u32[]{:S(2)}, u32[]{:S(2)}) collective-permute-start(bf16[2,384,256]{1,2,0:T(8,128)(2,1)} %pad_maximum_fusion), channel_id=1, source_target_pairs={{0,56},{8,64},{16,72},{24,80},{32,88},{40,96},{48,104},{56,112},{6... | collective-permute-start | bytes 1179656 | tf_op jit(solution)/shard_map/ppermute | solution.py:27
  45.6 45.3 %collective-permute-start.4 = (bf16[2,384,256]{1,2,0:T(8,128)(2,1)}, bf16[2,384,256]{1,2,0:T(8,128)(2,1)}, u32[]{:S(2)}, u32[]{:S(2)}) collective-permute-start(bf16[2,384,256]{1,2,0:T(8,128)(2,1)} %pad_maximum_fusion), channel_id=1, source_target_pairs={{0,8},{8,16},{16,24},{24,32},{32,40},{40,48},{48,56},{56,64},{64,7... | collective-permute-start | bytes 1179656 | tf_op jit(solution)/shard_map/ppermute | solution.py:27
  48.1 26.3 %collective-permute-start.1 = (bf16[2,384,256]{1,2,0:T(8,128)(2,1)}, bf16[2,384,256]{1,2,0:T(8,128)(2,1)}, u32[]{:S(2)}, u32[]{:S(2)}) collective-permute-start(bf16[2,384,256]{1,2,0:T(8,128)(2,1)} %pad_maximum_fusion), channel_id=1, source_target_pairs={{64,0},{72,8},{80,16},{88,24},{96,32},{104,40},{112,48},{120,56},{... | collective-permute-start | bytes 1179656 | tf_op jit(solution)/shard_map/ppermute | solution.py:27
  50.3 17.7 %collective-permute-start = (bf16[2,384,256]{1,2,0:T(8,128)(2,1)}, bf16[2,384,256]{1,2,0:T(8,128)(2,1)}, u32[]{:S(2)}, u32[]{:S(2)}) collective-permute-start(bf16[2,384,256]{1,2,0:T(8,128)(2,1)} %pad_maximum_fusion), channel_id=1, source_target_pairs={{72,0},{80,8},{88,16},{96,24},{104,32},{112,40},{120,48},{128,56},... | collective-permute-start | bytes 1179656 | tf_op jit(solution)/shard_map/ppermute | solution.py:27
  52.3 1557.6 %all-gather.6.cloned.1.call-start = ((), (), s32[]{:S(2)}) async-start(), calls=%async_computation.1 | async-start | bytes 6303744 | tf_op jit(solution)/shard_map/all_gather | solution.py:18
  64.3 26.5 %copy-start.5 = (bf16[384,2,128]{0,2,1:T(8,128)(2,1)S(1)}, bf16[384,2,128]{0,2,1:T(8,128)(2,1)}, u32[]{:S(2)}) copy-start(bf16[384,2,128]{0,2,1:T(8,128)(2,1)} %copy-done.4) | copy-start | bytes 589828
  68.0 16.8 %collective-permute-start.2 = (bf16[2,384,256]{1,2,0:T(8,128)(2,1)}, bf16[2,384,256]{1,2,0:T(8,128)(2,1)S(1)}, u32[]{:S(2)}, u32[]{:S(2)}) collective-permute-start(bf16[2,384,256]{1,2,0:T(8,128)(2,1)} %pad_maximum_fusion), channel_id=1, source_target_pairs={{56,0},{64,8},{72,16},{80,24},{88,32},{96,40},{104,48},{112,56},{1... | collective-permute-start | bytes 1179656 | tf_op jit(solution)/shard_map/ppermute | solution.py:27
  74.4 16.3 %collective-permute-start.3 = (bf16[2,384,256]{1,2,0:T(8,128)(2,1)}, bf16[2,384,256]{1,2,0:T(8,128)(2,1)S(1)}, u32[]{:S(2)}, u32[]{:S(2)}) collective-permute-start(bf16[2,384,256]{1,2,0:T(8,128)(2,1)} %pad_maximum_fusion), channel_id=1, source_target_pairs={{8,0},{16,8},{24,16},{32,24},{40,32},{48,40},{56,48},{64,56},{72,6... | collective-permute-start | bytes 1179656 | tf_op jit(solution)/shard_map/ppermute | solution.py:27
  84.8 10.7 collective-permute-start.7
  116.2 3.9 copy-start.27
  116.2 3.9 copy-start.26
  151.6 2.8 copy-start.8
  151.6 2.9 copy-start.23
  151.6 3.2 copy-start.31
  216.7 15.2 copy-start.24
  218.4 42.2 %copy-start.17 = (bf16[256,256]{0,1:T(8,128)(2,1)S(1)}, bf16[256,256]{0,1:T(8,128)(2,1)}, u32[]{:S(2)}) copy-start(bf16[256,256]{0,1:T(8,128)(2,1)} %copy.288) | copy-start | bytes 393220
  218.4 27.8 %collective-permute-start.8 = (bf16[2,384,256]{1,2,0:T(8,128)(2,1)}, bf16[2,384,256]{1,2,0:T(8,128)(2,1)}, u32[]{:S(2)}, u32[]{:S(2)}) collective-permute-start(bf16[2,384,256]{1,2,0:T(8,128)(2,1)} %get-tuple-element.399), channel_id=1, source_target_pairs={{0,72},{8,80},{16,88},{24,96},{32,104},{40,112},{48,120},{56,128},... | collective-permute-start | bytes 1179656 | tf_op jit(solution)/shard_map/ppermute | solution.py:27
  225.1 23.0 %collective-permute-start.15 = (bf16[2,384,256]{1,2,0:T(8,128)(2,1)}, bf16[2,384,256]{1,2,0:T(8,128)(2,1)}, u32[]{:S(2)}, u32[]{:S(2)}) collective-permute-start(bf16[2,384,256]{1,2,0:T(8,128)(2,1)} %get-tuple-element.400), channel_id=1, source_target_pairs={{72,0},{80,8},{88,16},{96,24},{104,32},{112,40},{120,48},{128,56},... | collective-permute-start | bytes 1179656 | tf_op jit(solution)/shard_map/ppermute | solution.py:27
  229.8 31.1 %copy-start.18 = (f32[256,256]{1,0:T(8,128)S(1)}, f32[256,256]{1,0:T(8,128)}, u32[]{:S(2)}) copy-start(f32[256,256]{1,0:T(8,128)} %copy.254) | copy-start | bytes 786436
  229.8 26.1 %collective-permute-start.14 = (bf16[2,384,256]{1,2,0:T(8,128)(2,1)}, bf16[2,384,256]{1,2,0:T(8,128)(2,1)}, u32[]{:S(2)}, u32[]{:S(2)}) collective-permute-start(bf16[2,384,256]{1,2,0:T(8,128)(2,1)} %get-tuple-element.401), channel_id=1, source_target_pairs={{64,0},{72,8},{80,16},{88,24},{96,32},{104,40},{112,48},{120,56},{... | collective-permute-start | bytes 1179656 | tf_op jit(solution)/shard_map/ppermute | solution.py:27
  232.6 293.9 %collective-permute-start.13 = (bf16[2,384,256]{1,2,0:T(8,128)(2,1)}, bf16[2,384,256]{1,2,0:T(8,128)(2,1)S(1)}, u32[]{:S(2)}, u32[]{:S(2)}) collective-permute-start(bf16[2,384,256]{1,2,0:T(8,128)(2,1)} %get-tuple-element.402), channel_id=1, source_target_pairs={{56,0},{64,8},{72,16},{80,24},{88,32},{96,40},{104,48},{112,56},{1... | collective-permute-start | bytes 1179656 | tf_op jit(solution)/shard_map/ppermute | solution.py:27
  236.3 290.3 %collective-permute-start.12 = (bf16[2,384,256]{1,2,0:T(8,128)(2,1)}, bf16[2,384,256]{1,2,0:T(8,128)(2,1)S(1)}, u32[]{:S(2)}, u32[]{:S(2)}) collective-permute-start(bf16[2,384,256]{1,2,0:T(8,128)(2,1)} %get-tuple-element.403), channel_id=1, source_target_pairs={{8,0},{16,8},{24,16},{32,24},{40,32},{48,40},{56,48},{64,56},{72,6... | collective-permute-start | bytes 1179656 | tf_op jit(solution)/shard_map/ppermute | solution.py:27
  246.2 280.3 %collective-permute-start.11 = (bf16[2,384,256]{1,2,0:T(8,128)(2,1)}, bf16[2,384,256]{1,2,0:T(8,128)(2,1)S(1)}, u32[]{:S(2)}, u32[]{:S(2)}) collective-permute-start(bf16[2,384,256]{1,2,0:T(8,128)(2,1)} %get-tuple-element.404), channel_id=1, source_target_pairs={{0,8},{8,16},{16,24},{24,32},{32,40},{40,48},{48,56},{56,64},{64,7... | collective-permute-start | bytes 1179656 | tf_op jit(solution)/shard_map/ppermute | solution.py:27
  248.1 278.4 %collective-permute-start.10 = (bf16[2,384,256]{1,2,0:T(8,128)(2,1)}, bf16[2,384,256]{1,2,0:T(8,128)(2,1)}, u32[]{:S(2)}, u32[]{:S(2)}) collective-permute-start(bf16[2,384,256]{1,2,0:T(8,128)(2,1)} %get-tuple-element.405), channel_id=1, source_target_pairs={{0,56},{8,64},{16,72},{24,80},{32,88},{40,96},{48,104},{56,112},{6... | collective-permute-start | bytes 1179656 | tf_op jit(solution)/shard_map/ppermute | solution.py:27
  255.9 270.7 %collective-permute-start.9 = (bf16[2,384,256]{1,2,0:T(8,128)(2,1)}, bf16[2,384,256]{1,2,0:T(8,128)(2,1)}, u32[]{:S(2)}, u32[]{:S(2)}) collective-permute-start(bf16[2,384,256]{1,2,0:T(8,128)(2,1)} %get-tuple-element.406), channel_id=1, source_target_pairs={{0,64},{8,72},{16,80},{24,88},{32,96},{40,104},{48,112},{56,120},{... | collective-permute-start | bytes 1179656 | tf_op jit(solution)/shard_map/ppermute | solution.py:27
  529.6 4.0 copy-start.7
  531.6 4.2 copy-start.3
  531.6 4.1 copy-start.19
  537.1 2.6 copy-start.21
  537.1 2.6 copy-start.22
  1609.8 11.0 copy-start.1
  (2 other events, 2.7 us)
Sparse Core Ops, SparseCore 0:
  52.4 83.1 all-gather.3
  156.4 1453.3 all-gather.5
